TPU v7x, 512 devices: a whole 4x8x8 slice. The times are simulated.
512 devices in a mesh: tm: 32 (over y, z_lo), row: 16 (over x, z_hi, core).
Axes of the slice: x: 4, y: 8, z: 8 (z_hi: 2, z_lo: 4; z = z_hi * 4 + z_lo), core: 2. Of those that a mesh axis runs over, the one named last changes fastest.
Arguments:
- latents: bfloat16 [64, 96, 80, 256], P('tm', 'row'), may hold values from -6 to 6
- conv_weight: bfloat16 [3, 3, 768, 256], replicated, may hold values from -0.078125 to 0.078125
- norm_gain: float32 [256], replicated, may hold values from 0.1 to 1.9
- depth_target: bfloat16 [64, 96, 80, 128], P('tm', 'row'), may hold values from -6 to 6
Outputs:
- features: bfloat16 [64, 96, 80, 256], P('tm', 'row')
- gram: float32 [256, 256], replicated
- cross: float32 [256, 128], replicated
All inputs are finite; a program needn't handle non-finite values.
Results may differ from a plain program's by a relative error of at most 0.003.
Values may be sent and summed in bfloat16 or wider, within the bound.
A program may use at most 64 MiB of HBM per device.

v0:
```python
import jax
import jax.numpy as jnp
from jax import lax
from jax.sharding import PartitionSpec as P


def from_behind(value, axis, steps):
    count = lax.axis_size(axis)
    first, last = (max(0, -steps), min(count, count - steps))
    return lax.ppermute(value, axis, [(source, source + steps) for source in range(first, last)])


def extended(cells, sides, width):
    for axis, dim in sides:
        count = lax.axis_size(axis)
        ends = count - 1
        head = lax.slice_in_dim(cells, 0, width, axis=dim)
        tail = lax.slice_in_dim(cells, cells.shape[dim] - width, cells.shape[dim], axis=dim)
        cells = jnp.concatenate(
            [
                lax.ppermute(tail, axis, [(i, (i + 1) % count) for i in range(ends)]),
                cells,
                lax.ppermute(head, axis, [((i + 1) % count, i) for i in range(ends)]),
            ],
            axis=dim,
        )
    return cells


def convolve(padded, conv_weight):
    frames = padded.shape[0] - 2
    rows = padded.shape[1] - 2
    cols = padded.shape[2]
    chans = conv_weight.shape[3]
    wide = jnp.pad(padded, ((0, 0), (0, 0), (1, 1), (0, 0)))
    stacked = jnp.concatenate(
        [wide[:, :, 0:cols], wide[:, :, 1 : cols + 1], wide[:, :, 2 : cols + 2]], axis=3
    )
    total = jnp.zeros((frames * rows * cols, chans), jnp.float32)
    for dtime in range(3):
        for drow in range(3):
            piece = stacked[dtime : dtime + frames, drow : drow + rows].reshape(
                frames * rows * cols, -1
            )
            total = total + jnp.dot(
                piece, conv_weight[dtime, drow], preferred_element_type=jnp.float32
            )
    return total


def on_device(latents, conv_weight, norm_gain, depth_target):
    cached = from_behind(latents, "tm", 1)
    joined = jnp.concatenate([cached, latents], axis=0)
    padded = extended(joined, (("row", 1),), 1)
    conv = convolve(padded, conv_weight)
    flat_in = latents.reshape(conv.shape[0], conv.shape[1]).astype(jnp.float32)
    normed = conv * jax.lax.rsqrt(jnp.mean(conv * conv, axis=1, keepdims=True) + 1e-06) * norm_gain
    flat = (flat_in + jax.nn.silu(normed)).astype(jnp.bfloat16)
    targets = depth_target.reshape(flat.shape[0], -1)
    gram_part = jnp.dot(flat.T, flat, preferred_element_type=jnp.float32)
    cross_part = jnp.dot(flat.T, targets, preferred_element_type=jnp.float32)
    count = flat.shape[0] * lax.axis_size("tm") * lax.axis_size("row")
    gram_sum, cross_sum = lax.psum((gram_part, cross_part), ("tm", "row"))
    return (flat.reshape(latents.shape), gram_sum / count, cross_sum / count)


def solution(mesh):
    in_specs = (P("tm", "row", None, None), P(), P(), P("tm", "row", None, None))
    out_specs = (P("tm", "row", None, None), P(), P())
    return jax.shard_map(
        on_device, mesh=mesh, in_specs=in_specs, out_specs=out_specs, check_vma=False
    )
```

profile of v0, /device:TPU:1, one launch (start us, length us, event | category | flops | bytes accessed | tf_op | source)
XLA Modules:
  0.0 338.9 jit_solution(941491397047165075)
XLA Ops:
  7.2 0.0 copy-start
  7.2 0.0 all-reduce.4.cloned.1.call-start
  7.2 5.0 %collective-permute-start = (bf16[2,6,80,256]{3,2,1,0:T(8,128)(2,1)}, bf16[2,6,80,256]{3,2,1,0:T(8,128)(2,1)S(1)}, u32[]{:S(2)}, u32[]{:S(2)}) collective-permute-start(bf16[2,6,80,256]{3,2,1,0:T(8,128)(2,1)} %param.4), channel_id=1, source_target_pairs={{0,16},{16,32},{32,48},{48,64},{64,80},{80,96},{96,112},{112,128},... | collective-permute-start | bytes 1474568 | tf_op jit(solution)/shard_map/ppermute | solution.py:10
  12.2 7.8 %collective-permute-done = bf16[2,6,80,256]{3,2,1,0:T(8,128)(2,1)S(1)} collective-permute-done((bf16[2,6,80,256]{3,2,1,0:T(8,128)(2,1)}, bf16[2,6,80,256]{3,2,1,0:T(8,128)(2,1)S(1)}, u32[]{:S(2)}, u32[]{:S(2)}) %collective-permute-start) | collective-permute-done | bytes 491552 | tf_op jit(solution)/shard_map/ppermute | solution.py:10
  20.1 1.1 constant_dynamic-update-slice_fusion
  21.2 13.5 %collective-permute-start.1 = (bf16[4,1,80,256]{3,2,1,0:T(8,128)(2,1)S(1)}, bf16[4,1,80,256]{3,2,1,0:T(8,128)(2,1)S(1)}, u32[]{:S(2)}, u32[]{:S(2)}) collective-permute-start(bf16[4,1,80,256]{3,2,1,0:T(8,128)(2,1)S(1)} %get-tuple-element.16), channel_id=1, source_target_pairs={{0,1},{1,2},{2,3},{3,4},{4,5},{5,6},{6,7},{7,8},{8,9},{9,10},{10,1... | collective-permute-start | bytes 491528 | tf_op jit(solution)/shard_map/ppermute | solution.py:21
  34.7 1.9 collective-permute-start.2
  36.6 2.1 collective-permute-done.1
  38.7 7.3 %collective-permute-done.2 = bf16[4,1,80,256]{3,2,1,0:T(8,128)(2,1)S(1)} collective-permute-done((bf16[4,1,80,256]{3,2,1,0:T(8,128)(2,1)S(1)}, bf16[4,1,80,256]{3,2,1,0:T(8,128)(2,1)S(1)}, u32[]{:S(2)}, u32[]{:S(2)}) %collective-permute-start.2) | collective-permute-done | bytes 163872 | tf_op jit(solution)/shard_map/ppermute | solution.py:23
  46.0 0.8 fusion.5
  46.7 0.9 fusion.41
  47.6 0.3 pad_maximum_fusion
  48.0 0.0 copy-start.1
  48.0 1.2 fusion.40
  49.2 0.7 copy-done.1
  50.0 0.5 fusion.14
  50.5 0.5 fusion.16
  51.1 0.5 fusion.18
  51.6 0.5 fusion.20
  52.2 0.5 fusion.22
  52.8 0.5 fusion.24
  53.3 0.5 fusion.26
  53.9 0.5 fusion.28
  54.4 0.0 copy-start.2
  54.4 0.0 copy-start.4
  54.5 0.9 multiply_reduce_fusion
  55.4 0.1 copy-done.2
  55.5 0.0 copy-done.4
  55.5 0.4 fusion.13
  55.9 0.0 copy-start.3
  55.9 1.1 fusion.43
  56.9 0.0 copy-done
  56.9 1.0 fusion.44
  57.9 0.0 all-reduce.4.cloned.1.call-update
  58.0 270.9 %all-reduce.4.cloned.1.call-done = (f32[256,256]{1,0:T(8,128)}, f32[256,128]{1,0:T(8,128)}) async-done(((f32[256,256]{1,0:T(8,128)}, f32[256,128]{1,0:T(8,128)}), (f32[256,256]{1,0:T(8,128)}, f32[256,128]{1,0:T(8,128)})) %all-reduce.4.cloned.1.call-update) | async-done | bytes 393232 | tf_op jit(solution)/shard_map/psum | solution.py:63
  328.8 1.7 broadcast_multiply_fusion
  330.5 0.0 copy-done.3
  330.5 1.6 broadcast_multiply_fusion.1
  (3 shorter events, 0.1 us)
Async XLA Ops:
  7.2 49.8 %copy-start = (bf16[2,6,80,128]{3,2,1,0:T(8,128)(2,1)S(1)}, bf16[2,6,80,128]{3,2,1,0:T(8,128)(2,1)}, u32[]{:S(2)}) copy-start(bf16[2,6,80,128]{3,2,1,0:T(8,128)(2,1)} %param.7) | copy-start | bytes 737284
  7.2 321.6 %all-reduce.4.cloned.1.call-start = ((), (), s32[]{:S(2)}) async-start(), calls=%async_computation | async-start | bytes 786432 | tf_op jit(solution)/shard_map/psum | solution.py:63
  7.2 12.8 %collective-permute-start = (bf16[2,6,80,256]{3,2,1,0:T(8,128)(2,1)}, bf16[2,6,80,256]{3,2,1,0:T(8,128)(2,1)S(1)}, u32[]{:S(2)}, u32[]{:S(2)}) collective-permute-start(bf16[2,6,80,256]{3,2,1,0:T(8,128)(2,1)} %param.4), channel_id=1, source_target_pairs={{0,16},{16,32},{32,48},{48,64},{64,80},{80,96},{96,112},{112,128},... | collective-permute-start | bytes 1474568 | tf_op jit(solution)/shard_map/ppermute | solution.py:10
  21.2 17.5 %collective-permute-start.1 = (bf16[4,1,80,256]{3,2,1,0:T(8,128)(2,1)S(1)}, bf16[4,1,80,256]{3,2,1,0:T(8,128)(2,1)S(1)}, u32[]{:S(2)}, u32[]{:S(2)}) collective-permute-start(bf16[4,1,80,256]{3,2,1,0:T(8,128)(2,1)S(1)} %get-tuple-element.16), channel_id=1, source_target_pairs={{0,1},{1,2},{2,3},{3,4},{4,5},{5,6},{6,7},{7,8},{8,9},{9,10},{10,1... | collective-permute-start | bytes 491528 | tf_op jit(solution)/shard_map/ppermute | solution.py:21
  34.7 11.3 %collective-permute-start.2 = (bf16[4,1,80,256]{3,2,1,0:T(8,128)(2,1)S(1)}, bf16[4,1,80,256]{3,2,1,0:T(8,128)(2,1)S(1)}, u32[]{:S(2)}, u32[]{:S(2)}) collective-permute-start(bf16[4,1,80,256]{3,2,1,0:T(8,128)(2,1)S(1)} %get-tuple-element.17), channel_id=1, source_target_pairs={{1,0},{2,1},{3,2},{4,3},{5,4},{6,5},{7,6},{8,7},{9,8},{10,9},{11,1... | collective-permute-start | bytes 491528 | tf_op jit(solution)/shard_map/ppermute | solution.py:23
  48.0 2.0 copy-start.1
  54.4 1.0 copy-start.2
  54.4 1.0 copy-start.4
  55.9 274.6 %copy-start.3 = (bf16[960,256]{1,0:T(8,128)(2,1)}, bf16[960,256]{1,0:T(8,128)(2,1)S(1)}, u32[]{:S(2)}) copy-start(bf16[960,256]{1,0:T(8,128)(2,1)S(1)} %fusion.13) | copy-start | bytes 1474564
Sparse Core Ops, SparseCore 0:
  58.1 270.6 all-reduce.3
where the time goes:
time: 339 us
  waiting for transfers between devices  288 us (85%)
  starting transfers between devices  20.4 us (6%)
  between operations  14.2 us (4%)
  matrix products  7.34 us (2%)
  other arithmetic  4.74 us (1%)
  local copies, waits for them, and re-layouts  4.12 us (1%)
    psum x1, waiting for transfers between devices, on_device(): gram_sum, cross_sum = lax.psum((gram_part, cross_part), ('tm', 'row'))  271 us
    ppermute x1, starting transfers between devices, extended(): lax.ppermute(tail, axis, [(i, (i + 1) % count) for i in range(ends)])  13.5 us
    ppermute x1, waiting for transfers between devices, from_behind(): lax.ppermute(value, axis, [(source, source + steps) for source in range(f...  7.81 us
    ppermute x1, waiting for transfers between devices, extended(): lax.ppermute(head, axis, [((i + 1) % count, i) for i in range(ends)])  7.3 us
  transfers between devices with their start and end apart: 4, of which 4 were waited for; matrix products, arithmetic and copies ran while one was open for 0% of the time, Pallas kernels for 0%

commit v1 on v0

--- a/solution.py
+++ b/solution.py
@@ -60,7 +60,7 @@
     gram_part = jnp.dot(flat.T, flat, preferred_element_type=jnp.float32)
     cross_part = jnp.dot(flat.T, targets, preferred_element_type=jnp.float32)
     count = flat.shape[0] * lax.axis_size("tm") * lax.axis_size("row")
-    gram_sum, cross_sum = lax.psum((gram_part, cross_part), ("tm", "row"))
+    gram_sum, cross_sum = lax.psum(lax.psum((gram_part, cross_part), "tm"), "row")
     return (flat.reshape(latents.shape), gram_sum / count, cross_sum / count)
 
 

time: 339 us -> 556 us (1.64)
  waiting for transfers between devices: 288 us -> 505 us
    psum x1 -> x2, waiting for transfers between devices: 271 us -> 488 us  [the longest x1 281 us: on_device(): lax.psum((gram_part, cross_part), 'tm')]
  transfers between devices with their start and end apart: 4 -> 5, of which waited for: 4 -> 5; matrix products, arithmetic and copies ran while one was open for 0% -> 0% of each run, Pallas kernels for 0% -> 0%
where the time goes in v1:
time: 556 us
  waiting for transfers between devices  505 us (91%)
  starting transfers between devices  20.5 us (4%)
  between operations  14.2 us (3%)
  matrix products  7.34 us (1%)
    psum x1, waiting for transfers between devices, on_device(): lax.psum((gram_part, cross_part), 'tm')  281 us
    psum x1, waiting for transfers between devices, on_device(): lax.psum(lax.psum((gram_part, cross_part), 'tm'), 'row')  207 us
    ppermute x1, starting transfers between devices, extended(): lax.ppermute(tail, axis, [(i, (i + 1) % count) for i in range(ends)])  13.5 us
  transfers between devices with their start and end apart: 5, of which 5 were waited for; matrix products, arithmetic and copies ran while one was open for 0% of the time, Pallas kernels for 0%

profile of v1, /device:TPU:1, one launch (start us, length us, event | category | flops | bytes accessed | tf_op | source)
XLA Modules:
  0.0 555.8 jit_solution(18262894178746923875)
XLA Ops:
  7.2 0.0 copy-start
  7.2 0.0 all-reduce.6.cloned.1.call-start
  7.2 5.0 collective-permute-start
  12.2 7.8 %collective-permute-done = bf16[2,6,80,256]{3,2,1,0:T(8,128)(2,1)S(1)} collective-permute-done((bf16[2,6,80,256]{3,2,1,0:T(8,128)(2,1)}, bf16[2,6,80,256]{3,2,1,0:T(8,128)(2,1)S(1)}, u32[]{:S(2)}, u32[]{:S(2)}) %collective-permute-start) | collective-permute-done | bytes 491552 | tf_op jit(solution)/shard_map/ppermute | solution.py:10
  20.1 1.1 constant_dynamic-update-slice_fusion
  21.2 13.5 %collective-permute-start.1 = (bf16[4,1,80,256]{3,2,1,0:T(8,128)(2,1)S(1)}, bf16[4,1,80,256]{3,2,1,0:T(8,128)(2,1)S(1)}, u32[]{:S(2)}, u32[]{:S(2)}) collective-permute-start(bf16[4,1,80,256]{3,2,1,0:T(8,128)(2,1)S(1)} %get-tuple-element.18), channel_id=1, source_target_pairs={{0,1},{1,2},{2,3},{3,4},{4,5},{5,6},{6,7},{7,8},{8,9},{9,10},{10,1... | collective-permute-start | bytes 491528 | tf_op jit(solution)/shard_map/ppermute | solution.py:21
  34.7 1.9 collective-permute-start.2
  36.6 2.1 collective-permute-done.1
  38.7 7.3 %collective-permute-done.2 = bf16[4,1,80,256]{3,2,1,0:T(8,128)(2,1)S(1)} collective-permute-done((bf16[4,1,80,256]{3,2,1,0:T(8,128)(2,1)S(1)}, bf16[4,1,80,256]{3,2,1,0:T(8,128)(2,1)S(1)}, u32[]{:S(2)}, u32[]{:S(2)}) %collective-permute-start.2) | collective-permute-done | bytes 163872 | tf_op jit(solution)/shard_map/ppermute | solution.py:23
  46.0 0.8 fusion.5
  46.7 0.9 fusion.41
  47.6 0.3 pad_maximum_fusion
  48.0 0.0 copy-start.1
  48.0 1.2 fusion.40
  49.2 0.7 copy-done.1
  50.0 0.5 fusion.14
  50.5 0.5 fusion.16
  51.1 0.5 fusion.18
  51.6 0.5 fusion.20
  52.2 0.5 fusion.22
  52.8 0.5 fusion.24
  53.3 0.5 fusion.26
  53.9 0.5 fusion.28
  54.4 0.0 copy-start.2
  54.4 0.0 copy-start.4
  54.5 0.9 multiply_reduce_fusion
  55.4 0.1 copy-done.2
  55.5 0.0 copy-done.4
  55.5 0.4 fusion.13
  55.9 0.0 copy-start.3
  55.9 1.1 fusion.43
  56.9 0.0 copy-done
  56.9 1.0 fusion.44
  57.9 0.0 all-reduce.6.cloned.1.call-update
  58.0 0.0 all-reduce.8.cloned.1.call-start
  58.0 280.6 %all-reduce.6.cloned.1.call-done = (f32[256,256]{1,0:T(8,128)}, f32[256,128]{1,0:T(8,128)}) async-done(((f32[256,256]{1,0:T(8,128)}, f32[256,128]{1,0:T(8,128)}), (f32[256,256]{1,0:T(8,128)}, f32[256,128]{1,0:T(8,128)})) %all-reduce.6.cloned.1.call-update) | async-done | bytes 393232 | tf_op jit(solution)/shard_map/psum | solution.py:63
  338.6 0.0 all-reduce.8.cloned.1.call-update
  338.6 207.1 %all-reduce.8.cloned.1.call-done = (f32[256,256]{1,0:T(8,128)}, f32[256,128]{1,0:T(8,128)}) async-done(((f32[256,256]{1,0:T(8,128)}, f32[256,128]{1,0:T(8,128)}), (f32[256,256]{1,0:T(8,128)}, f32[256,128]{1,0:T(8,128)})) %all-reduce.8.cloned.1.call-update) | async-done | bytes 393232 | tf_op jit(solution)/shard_map/psum | solution.py:63
  545.7 1.7 broadcast_multiply_fusion
  547.4 0.0 copy-done.3
  547.4 1.6 broadcast_multiply_fusion.1
  (3 shorter events, 0.1 us)
Async XLA Ops:
  7.2 49.8 %copy-start = (bf16[2,6,80,128]{3,2,1,0:T(8,128)(2,1)S(1)}, bf16[2,6,80,128]{3,2,1,0:T(8,128)(2,1)}, u32[]{:S(2)}) copy-start(bf16[2,6,80,128]{3,2,1,0:T(8,128)(2,1)} %param.7) | copy-start | bytes 737284
  7.2 331.4 %all-reduce.6.cloned.1.call-start = ((), (), s32[]{:S(2)}) async-start(), calls=%async_computation | async-start | bytes 786432 | tf_op jit(solution)/shard_map/psum | solution.py:63
  7.2 12.8 %collective-permute-start = (bf16[2,6,80,256]{3,2,1,0:T(8,128)(2,1)}, bf16[2,6,80,256]{3,2,1,0:T(8,128)(2,1)S(1)}, u32[]{:S(2)}, u32[]{:S(2)}) collective-permute-start(bf16[2,6,80,256]{3,2,1,0:T(8,128)(2,1)} %param.4), channel_id=1, source_target_pairs={{0,16},{16,32},{32,48},{48,64},{64,80},{80,96},{96,112},{112,128},... | collective-permute-start | bytes 1474568 | tf_op jit(solution)/shard_map/ppermute | solution.py:10
  21.2 17.5 %collective-permute-start.1 = (bf16[4,1,80,256]{3,2,1,0:T(8,128)(2,1)S(1)}, bf16[4,1,80,256]{3,2,1,0:T(8,128)(2,1)S(1)}, u32[]{:S(2)}, u32[]{:S(2)}) collective-permute-start(bf16[4,1,80,256]{3,2,1,0:T(8,128)(2,1)S(1)} %get-tuple-element.18), channel_id=1, source_target_pairs={{0,1},{1,2},{2,3},{3,4},{4,5},{5,6},{6,7},{7,8},{8,9},{9,10},{10,1... | collective-permute-start | bytes 491528 | tf_op jit(solution)/shard_map/ppermute | solution.py:21
  34.7 11.3 %collective-permute-start.2 = (bf16[4,1,80,256]{3,2,1,0:T(8,128)(2,1)S(1)}, bf16[4,1,80,256]{3,2,1,0:T(8,128)(2,1)S(1)}, u32[]{:S(2)}, u32[]{:S(2)}) collective-permute-start(bf16[4,1,80,256]{3,2,1,0:T(8,128)(2,1)S(1)} %get-tuple-element.19), channel_id=1, source_target_pairs={{1,0},{2,1},{3,2},{4,3},{5,4},{6,5},{7,6},{8,7},{9,8},{10,9},{11,1... | collective-permute-start | bytes 491528 | tf_op jit(solution)/shard_map/ppermute | solution.py:23
  48.0 2.0 copy-start.1
  54.4 1.0 copy-start.2
  54.4 1.0 copy-start.4
  55.9 491.5 %copy-start.3 = (bf16[960,256]{1,0:T(8,128)(2,1)}, bf16[960,256]{1,0:T(8,128)(2,1)S(1)}, u32[]{:S(2)}) copy-start(bf16[960,256]{1,0:T(8,128)(2,1)S(1)} %fusion.13) | copy-start | bytes 1474564
  58.0 487.8 %all-reduce.8.cloned.1.call-start = ((), (), s32[]{:S(2)}) async-start(), calls=%async_computation.1 | async-start | bytes 786432 | tf_op jit(solution)/shard_map/psum | solution.py:63
Sparse Core Ops, SparseCore 0:
  58.1 280.4 all-reduce.5
  341.5 204.1 all-reduce.7
